TPU v7x, 1024 devices: a whole 8x8x8 slice. The times are simulated.
1024 devices in a mesh: seq: 64 (over x, y_lo, core), chan: 16 (over y_hi, z).
Axes of the slice: x: 8, y: 8 (y_hi: 2, y_lo: 4; y = y_hi * 4 + y_lo), z: 8, core: 2. Of those that a mesh axis runs over, the one named last changes fastest.
Arguments:
- features: bfloat16 [16384, 3, 8192], P(('seq', 'chan')), may hold values from -6 to 6
- short_taps: float32 [7, 3, 8192], P(None, None, 'chan'), may hold values from -2 to 2
- mr_filter: float32 [512, 128], P('chan'), may hold values from -0.5 to 0.5
- out_weight: bfloat16 [8192, 4096], P('chan', 'seq'), may hold values from -0.1875 to 0.1875
- residual: bfloat16 [16384, 4096], P('seq', 'chan'), may hold values from -6 to 6
Outputs:
- block_out: bfloat16 [16384, 4096], P('seq', 'chan')
All inputs are finite; a program needn't handle non-finite values.
Results may differ from a plain program's by a relative error of at most 0.015.
Values may be sent and summed in bfloat16 or wider, within the bound.
No kernel may reach another device: no remote copies, remote signals or barrier semaphores. Data moves between devices by JAX's collectives and lax.ppermute only.
A program may use at most 64 MiB of HBM per device.

v0:
```python
import jax
import jax.numpy as jnp
from jax import lax
from jax.sharding import PartitionSpec as P

KS = 7
KMR = 128


def passed_along(block, axis, distance):
    devices = range(lax.axis_size(axis))
    route = [(i - distance, i) for i in devices if i - distance in devices]
    return lax.ppermute(block, axis, route)


def short_filter(padded, tap_table, out_count):
    widened = padded.astype(jnp.float32)
    result = jnp.zeros((out_count,) + widened.shape[1:], jnp.float32)
    for offset in range(KS):
        first_row = KS - 1 - offset
        result = result + tap_table[offset] * widened[first_row : first_row + out_count]
    return result


def band_tables(filters):
    tap_span = filters.shape[1]
    later_pos = jnp.arange(tap_span, dtype=jnp.int32)[:, None, None]
    earlier_pos = jnp.arange(tap_span, dtype=jnp.int32)[None, :, None]
    lag_pos = jnp.arange(tap_span, dtype=jnp.int32)[None, None, :]
    near_pick = (lag_pos == later_pos - earlier_pos).astype(jnp.float32)
    far_pick = (lag_pos == later_pos - earlier_pos + tap_span).astype(jnp.float32)
    near_band = jnp.einsum("tsj,gj->gts", near_pick, filters, precision=lax.Precision.HIGHEST)
    far_band = jnp.einsum("tsj,gj->gts", far_pick, filters, precision=lax.Precision.HIGHEST)
    return (near_band, far_band)


def medium_conv(extended, filters):
    total_rows, chan_count = extended.shape
    groups = filters.shape[0]
    group_size = chan_count // groups
    blocks = extended.reshape(total_rows // KMR, KMR, groups, group_size)
    near_band, far_band = band_tables(filters)
    result = jnp.einsum("gts,nsgc->ntgc", near_band, blocks[1:], precision=lax.Precision.HIGHEST)
    result = result + jnp.einsum(
        "gts,nsgc->ntgc", far_band, blocks[:-1], precision=lax.Precision.HIGHEST
    )
    return result.reshape(-1, chan_count)


def body(features, short_taps, mr_filter, out_weight, residual):
    local_rows = lax.all_to_all(features, "chan", split_axis=2, concat_axis=0, tiled=True)
    row_count = local_rows.shape[0]
    chan_count = local_rows.shape[2]
    short_rows = passed_along(local_rows[row_count - (KS - 1) :], "seq", 1)
    short_out = short_filter(
        jnp.concatenate([short_rows, local_rows], axis=0), short_taps, row_count
    )
    query_short = short_out[:, 0, :]
    inner_local = short_out[:, 1, :] * short_out[:, 2, :]
    inner_rows = passed_along(
        inner_local[row_count - (KMR - 1) :].astype(jnp.bfloat16), "seq", 1
    ).astype(jnp.float32)
    inner_term = jnp.concatenate([inner_rows, inner_local], axis=0)
    extended = jnp.concatenate([jnp.zeros((1, chan_count), jnp.float32), inner_term], axis=0)
    mixed_out = medium_conv(extended, mr_filter)
    gated_out = (query_short * mixed_out).astype(jnp.bfloat16)
    partial_value = jnp.dot(
        gated_out,
        lax.all_gather(out_weight, "seq", axis=1, tiled=True),
        preferred_element_type=jnp.float32,
    )
    summed = lax.psum_scatter(
        partial_value.astype(jnp.bfloat16), "chan", scatter_dimension=1, tiled=True
    ).astype(jnp.float32)
    return (residual.astype(jnp.float32) + summed).astype(jnp.bfloat16)


def solution(mesh):
    placed = (
        P(("seq", "chan"), None, None),
        P(None, None, "chan"),
        P("chan", None),
        P("chan", "seq"),
        P("seq", "chan"),
    )
    return jax.shard_map(
        body, mesh=mesh, in_specs=placed, out_specs=P("seq", "chan"), check_vma=False
    )
```

profile of v0, /device:TPU:2, one launch (start us, length us, event | category | flops | bytes accessed | tf_op | source)
XLA Modules:
  0.0 405.9 jit_solution(13300999269399157465)
XLA Ops:
  6.5 0.7 all-gather.2.cloned.1.call-update
  7.3 9.9 %copy.22 = bf16[16,3,8192]{0,1,2:T(4,128)(2,1)} copy(bf16[16,3,8192]{2,0,1:T(8,128)(2,1)} %param.5) | data formatting | bytes 1572864 | tf_op args[0]
  17.2 13.6 %reshape.43 = bf16[16,2,12288]{2,1,0:T(2,128)(2,1)} reshape(bf16[8192,3,16]{2,1,0:T(4,128)(2,1)} %bitcast.62) | data formatting | bytes 1572864
  30.8 22.5 %all-to-all-start = ((bf16[16,2,12288]{2,1,0:T(2,128)(2,1)}), bf16[16,2,12288]{2,1,0:T(2,128)(2,1)S(1)}, u32[]{:S(2)}, u32[]{:S(2)}) async-start(bf16[16,2,12288]{2,1,0:T(2,128)(2,1)} %reshape.43), calls=%async_computation | async-start | bytes 1572864 | tf_op jit(solution)/shard_map/all_to_all | solution.py:51
  53.4 0.0 reduce-scatter.2.cloned.1.call-start
  53.4 0.0 copy-start.3
  53.5 7.3 %fusion.8 = f32[32,128,128,1]{2,0,1,3:T(8,128)} fusion(s32[128,128]{1,0:T(8,128)S(1)} %broadcast_add_fusion, f32[32,128]{1,0:T(8,128)S(1)} %copy-done), kind=kOutput, calls=%fused_computation.11 | convolution fusion | flops 807403520 | bytes 2179072 | tf_op jit(solution)/shard_map/tsj,gj->gts/dot_general | solution.py:33
  60.9 13.8 %all-to-all-done = bf16[16,2,12288]{2,1,0:T(2,128)(2,1)S(1)} async-done(((bf16[16,2,12288]{2,1,0:T(2,128)(2,1)}), bf16[16,2,12288]{2,1,0:T(2,128)(2,1)S(1)}, u32[]{:S(2)}, u32[]{:S(2)}) %all-to-all-start) | async-done | bytes 786464 | tf_op jit(solution)/shard_map/all_to_all | solution.py:51
  74.6 10.7 %reshape.44 = bf16[8192,3,16]{2,1,0:T(4,128)(2,1)} reshape(bf16[16,2,12288]{2,1,0:T(2,128)(2,1)S(1)} %all-to-all-done) | data formatting | bytes 1572864
  85.4 10.5 %copy.36 = bf16[16,3,16,512]{3,0,2,1:T(8,128)(2,1)S(1)} copy(bf16[16,3,16,512]{0,1,3,2:T(4,128)(2,1)} %bitcast.61) | data formatting | bytes 1572864 | tf_op jit(solution)/shard_map/all_to_all | solution.py:51
  95.9 1.9 collective-permute-start
  97.8 7.3 %fusion.9 = f32[32,128,128,1]{2,0,1,3:T(8,128)} fusion(s32[128,128]{1,0:T(8,128)S(1)} %iota_subtract_fusion, f32[32,128]{1,0:T(8,128)S(1)} %copy-done), kind=kOutput, calls=%fused_computation.12 | convolution fusion | flops 807403520 | bytes 2179072 | tf_op jit(solution)/shard_map/tsj,gj->gts/dot_general | solution.py:32
  105.2 0.2 maximum_convert_fusion
  105.4 1.3 fusion.10
  106.7 0.1 slice_multiply_fusion.7
  106.8 0.2 copy.25
  107.1 8.3 %collective-permute-start.1 = (bf16[127,512]{1,0:T(8,128)(2,1)S(1)}, bf16[127,512]{1,0:T(8,128)(2,1)S(1)}, u32[]{:S(2)}, u32[]{:S(2)}) collective-permute-start(bf16[127,512]{1,0:T(8,128)(2,1)S(1)} %fusion.27), channel_id=1, source_target_pairs={{0,16},{16,32},{32,48},{48,64},{64,80},{80,96},{96,112},{112,128},... | collective-permute-start | bytes 390152 | tf_op jit(solution)/shard_map/ppermute | solution.py:13
  115.4 0.3 mul.105
  115.6 0.1 fusion.32
  115.7 0.8 collective-permute-done.1
  116.5 0.1 pad_maximum_fusion
  116.6 0.2 copy.28
  116.8 0.3 slice.87
  117.1 6.0 %fusion.4 = f32[32,2,16,128]{3,2,1,0:T(8,128)S(1)} fusion(f32[32,128,128,1]{2,0,1,3:T(8,128)} %fusion.8, f32[2,128,32,16]{1,0,3,2:T(2,128)S(1)} %slice.87), kind=kOutput, calls=%fused_computation.7 | convolution fusion | flops 201326592 | bytes 3145728 | tf_op jit(solution)/shard_map/gts,nsgc->ntgc/dot_general | solution.py:44
  123.1 4.2 %fusion.19 = f32[2,128,32,16]{1,3,0,2:T(8,128)S(1)} fusion(f32[32,2,16,128]{3,2,1,0:T(8,128)S(1)} %fusion.4, f32[32,128,128,1]{2,0,1,3:T(8,128)S(1)} %copy-done.1, f32[2,128,32,16]{1,0,3,2:T(2,128)S(1)} %mul.105), kind=kOutput, calls=%fused_computation.27 | convolution fusion | flops 201457664 | bytes 3670016 | tf_op jit(solution)/shard_map/gts,nsgc->ntgc/dot_general | solution.py:43
  127.4 0.3 copy.31
  127.7 0.2 copy.32
  127.9 27.6 %all-gather.2.cloned.1.call-done = bf16[512,4096]{0,1:T(8,128)(2,1)} async-done(((bf16[512,64]{0,1:T(8,128)(2,1)}), bf16[512,4096]{0,1:T(8,128)(2,1)}) %all-gather.2.cloned.1.call-update) | async-done | bytes 4194320 | tf_op jit(solution)/shard_map/all_gather | solution.py:69
  155.5 4.8 %convolution_convert_fusion = bf16[256,4096]{1,0:T(8,128)(2,1)} fusion(bf16[512,4096]{0,1:T(8,128)(2,1)} %all-gather.2.cloned.1.call-done, f32[256,512]{1,0:T(8,128)S(1)} %copy.32, f32[256,3,512]{2,0,1:T(8,128)S(1)} %fusion.10), kind=kOutput, calls=%fused_computation.4 | convolution fusion | flops 1075052544 | bytes 7340032 | tf_op jit(solution)/shard_map/dot_general | solution.py:67
  160.3 0.0 reduce-scatter.2.cloned.1.call-update
  160.4 237.1 %reduce-scatter.2.cloned.1.call-done = bf16[256,256]{1,0:T(8,128)(2,1)} async-done(((bf16[256,4096]{1,0:T(8,128)(2,1)}), bf16[256,256]{1,0:T(8,128)(2,1)}) %reduce-scatter.2.cloned.1.call-update) | async-done | bytes 131088 | tf_op jit(solution)/shard_map/reduce_scatter | solution.py:72
  397.5 1.6 add_convert_fusion
  (25 shorter events, 0.2 us)
Async XLA Ops:
  6.5 46.9 %copy-start = (f32[32,128]{1,0:T(8,128)S(1)}, f32[32,128]{1,0:T(8,128)}, u32[]{:S(2)}) copy-start(f32[32,128]{1,0:T(8,128)} %param.7) | copy-start | bytes 49156
  6.5 149.0 %all-gather.2.cloned.1.call-start = ((), (), s32[]{:S(2)}) async-start(), calls=%async_computation.2 | async-start | bytes 4259840 | tf_op jit(solution)/shard_map/all_gather | solution.py:69
  30.8 43.8 %all-to-all-start = ((bf16[16,2,12288]{2,1,0:T(2,128)(2,1)}), bf16[16,2,12288]{2,1,0:T(2,128)(2,1)S(1)}, u32[]{:S(2)}, u32[]{:S(2)}) async-start(bf16[16,2,12288]{2,1,0:T(2,128)(2,1)} %reshape.43), calls=%async_computation | async-start | bytes 1572864 | tf_op jit(solution)/shard_map/all_to_all | solution.py:51
  53.4 344.1 %reduce-scatter.2.cloned.1.call-start = ((), (), s32[]{:S(2)}) async-start(), calls=%async_computation.3 | async-start | bytes 2228224 | tf_op jit(solution)/shard_map/reduce_scatter | solution.py:72
  53.4 7.3 %copy-start.3 = (f32[7,3,512]{2,0,1:T(8,128)S(1)}, f32[7,3,512]{2,0,1:T(8,128)}, u32[]{:S(2)}) copy-start(f32[7,3,512]{2,0,1:T(8,128)} %param.6) | copy-start | bytes 129028
  95.9 9.3 %collective-permute-start = (bf16[6,3,512]{2,0,1:T(8,128)(2,1)S(1)}, bf16[6,3,512]{2,0,1:T(8,128)(2,1)S(1)}, u32[]{:S(2)}, u32[]{:S(2)}) collective-permute-start(bf16[6,3,512]{2,0,1:T(8,128)(2,1)S(1)} %slice.88), channel_id=1, source_target_pairs={{0,16},{16,32},{32,48},{48,64},{64,80},{80,96},{96,112},{112,128},... | collective-permute-start | bytes 55304 | tf_op jit(solution)/shard_map/ppermute | solution.py:13
  105.2 1.5 copy-start.4
  107.0 9.5 %slice-start = ((f32[384]{0:T(512)}), f32[256]{0:T(256)S(1)}, s32[]{:S(2)}) async-start(f32[384]{0:T(512)} %copy-done.4), calls=%async_computation.4 | async-start | bytes 2048 | tf_op jit(solution)/shard_map/slice | solution.py:45
  107.1 9.4 %collective-permute-start.1 = (bf16[127,512]{1,0:T(8,128)(2,1)S(1)}, bf16[127,512]{1,0:T(8,128)(2,1)S(1)}, u32[]{:S(2)}, u32[]{:S(2)}) collective-permute-start(bf16[127,512]{1,0:T(8,128)(2,1)S(1)} %fusion.27), channel_id=1, source_target_pairs={{0,16},{16,32},{32,48},{48,64},{64,80},{80,96},{96,112},{112,128},... | collective-permute-start | bytes 390152 | tf_op jit(solution)/shard_map/ppermute | solution.py:13
  117.1 6.0 %copy-start.1 = (f32[32,128,128,1]{2,0,1,3:T(8,128)S(1)}, f32[32,128,128,1]{2,0,1,3:T(8,128)}, u32[]{:S(2)}) copy-start(f32[32,128,128,1]{2,0,1,3:T(8,128)} %fusion.9) | copy-start | bytes 6291460
  160.3 237.2 %copy-start.2 = (bf16[256,256]{1,0:T(8,128)(2,1)S(1)}, bf16[256,256]{1,0:T(8,128)(2,1)}, u32[]{:S(2)}) copy-start(bf16[256,256]{1,0:T(8,128)(2,1)} %param.9) | copy-start | bytes 393220
Sparse Core Ops, SparseCore 0:
  10.1 145.3 all-gather.1
  161.1 236.3 reduce-scatter.1
where the time goes:
time: 407 us; the launch traced here: 406 us
  waiting for transfers between devices  280 us (69%)
  local copies, waits for them, and re-layouts  46.4 us (11%)
  starting transfers between devices  32.8 us (8%)
  matrix products  29.7 us (7%)
  between operations  13.7 us (3%)
    reduce_scatter x1, waiting for transfers between devices, body(): lax.psum_scatter(partial_value.astype(jnp.bfloat16), 'chan', scatter_dime...  237 us
    unnamed x18, local copies, waits for them, and re-layouts  34.4 us
    all_gather x1, waiting for transfers between devices, body(): lax.all_gather(out_weight, 'seq', axis=1, tiled=True)  27.6 us
    all_to_all x1, starting transfers between devices, body(): lax.all_to_all(features, 'chan', split_axis=2, concat_axis=0, tiled=True)  22.5 us
    all_to_all x1, waiting for transfers between devices, body(): lax.all_to_all(features, 'chan', split_axis=2, concat_axis=0, tiled=True)  13.8 us
    all_to_all x1, local copies, waits for them, and re-layouts, body(): lax.all_to_all(features, 'chan', split_axis=2, concat_axis=0, tiled=True)  10.5 us
    ppermute x2, starting transfers between devices, passed_along(): return lax.ppermute(block, axis, route)  10.2 us
  transfers between devices with their start and end apart: 5, of which 4 were waited for; matrix products, arithmetic and copies ran while one was open for 18% of the time, Pallas kernels for 0%

commit v1 on v0

v1 whole, which is shorter than its diff:
```python
import jax
import jax.numpy as jnp
from jax import lax
from jax.experimental import pallas as pl
from jax.experimental.pallas import tpu as pltpu
from jax.sharding import Mesh
from jax.sharding import PartitionSpec as P

KS = 7
KMR = 128
GROUP = 16
LANES = 128
INTERPRET = False

SEQ = ("x", "yh", "yl", "core")
CHAN = ("Y", "zz", "par")


def call(kernel, flops=0, moved=0, vmem_mib=16, **kwargs):
    cost = pl.CostEstimate(flops=flops, bytes_accessed=moved, transcendentals=0)
    params = pltpu.CompilerParams(vmem_limit_bytes=vmem_mib << 20)
    return pl.pallas_call(
        kernel, interpret=INTERPRET, cost_estimate=cost, compiler_params=params, **kwargs
    )


def bands_kernel(filter_ref, band_ref):
    row = lax.broadcasted_iota(jnp.int32, (KMR, KMR), 0)
    lane = lax.broadcasted_iota(jnp.int32, (KMR, KMR), 1)
    for group in range(filter_ref.shape[0]):
        taps = jnp.broadcast_to(filter_ref[group : group + 1, :], (KMR, KMR))
        rolled = pltpu.roll(taps, 0, 1, stride=1, stride_axis=0)
        band_ref[group, :KMR, :] = jnp.where(lane < row, rolled, 0.0).astype(band_ref.dtype)
        band_ref[group, KMR:, :] = jnp.where(lane >= row, rolled, 0.0).astype(band_ref.dtype)


def short_rows(ext_ref, taps, first, count):
    total = taps[0:1] * ext_ref[first : first + count, :]
    for offset in range(1, KS):
        total = total + taps[offset : offset + 1] * ext_ref[first - offset : first - offset + count, :]
    return total


def conv_kernel(rows_ref, halo_ref, taps_ref, band_ref, gated_ref, q_ext, k_ext, v_ext, inner_t, mixed_t):
    sources, _, block, _ = rows_ref.shape
    tokens = sources * block
    halo_blocks = (halo_ref.shape[0] - 1) // 2
    halo = halo_blocks * block
    q_ext[:block, :] = halo_ref[2 * halo_blocks].astype(jnp.float32)
    for i in range(halo_blocks):
        k_ext[i * block : (i + 1) * block, :] = halo_ref[2 * i].astype(jnp.float32)
        v_ext[i * block : (i + 1) * block, :] = halo_ref[2 * i + 1].astype(jnp.float32)
    for i in range(sources):
        q_ext[block + i * block : block + (i + 1) * block, :] = rows_ref[i, 0].astype(jnp.float32)
        k_ext[halo + i * block : halo + (i + 1) * block, :] = rows_ref[i, 1].astype(jnp.float32)
        v_ext[halo + i * block : halo + (i + 1) * block, :] = rows_ref[i, 2].astype(jnp.float32)
    taps_q, taps_k, taps_v = (taps_ref[i] for i in range(3))
    for i in range(tokens // KMR + 1):
        first = halo - KMR + i * KMR
        inner = short_rows(k_ext, taps_k, first, KMR) * short_rows(v_ext, taps_v, first, KMR)
        inner_t[:, i * KMR : (i + 1) * KMR] = inner.T.astype(inner_t.dtype)
    spans = tokens // KMR
    for group in range(band_ref.shape[0]):
        chans = slice(group * GROUP, (group + 1) * GROUP)
        pieces = [inner_t[chans, i * KMR : (i + 2) * KMR] for i in range(spans)]
        out = jnp.dot(
            jnp.concatenate(pieces, axis=0), band_ref[group], preferred_element_type=jnp.float32
        )
        for i in range(spans):
            mixed_t[chans, i * KMR : (i + 1) * KMR] = out[i * GROUP : (i + 1) * GROUP]
    for i in range(spans):
        query = short_rows(q_ext, taps_q, block + i * KMR, KMR)
        mixed = mixed_t[:, i * KMR : (i + 1) * KMR].T
        gated_ref[i * KMR : (i + 1) * KMR, :] = (query * mixed).astype(gated_ref.dtype)


def project_kernel(par_ref, own_ref, pair_ref, mine_ref, other_ref, out_ref, both):
    @pl.when(pl.program_id(0) == 0)
    def _():
        par = par_ref[0]
        both[par] = own_ref[...]
        both[1 - par] = pair_ref[...]

    total = None
    for b in range(2):
        pieces = []
        for yl in range(mine_ref.shape[2]):
            pieces += [mine_ref[0, b, yl], other_ref[0, b, yl]]
        term = lax.dot_general(
            both[b],
            jnp.concatenate(pieces, axis=0),
            (((1,), (1,)), ((), ())),
            preferred_element_type=jnp.float32,
        )
        total = term if total is None else total + term
    out_ref[0] = total.astype(out_ref.dtype)


def sum_kernel(core_ref, parts_ref, residual_ref, out_ref):
    total = parts_ref[0].astype(jnp.float32)
    for i in range(1, parts_ref.shape[0]):
        total = total + parts_ref[i].astype(jnp.float32)
    for i in range(total.shape[1] // LANES):
        lanes = slice(i * LANES, (i + 1) * LANES)
        piece = total[:, lanes]
        piece = jnp.where(core_ref[0] == 0, piece, pltpu.roll(piece, LANES // 2, 1))
        out_ref[:, lanes] = (residual_ref[:, lanes].astype(jnp.float32) + piece).astype(out_ref.dtype)


def body(features, short_taps, mr_filter, out_weight, residual):
    block, _, width = features.shape
    sources = lax.axis_size(CHAN)
    chans = width // sources
    tokens = sources * block
    bf16, f32 = jnp.bfloat16, jnp.float32
    vmem = pl.BlockSpec(memory_space=pltpu.VMEM)
    smem = pl.BlockSpec(memory_space=pltpu.SMEM)

    weight = lax.ppermute(out_weight.T, ("yh", "par"), [(0, 0), (1, 2), (2, 1), (3, 3)])
    cols = weight.shape[0]
    near = lax.all_gather(weight, ("yh", "yl"), axis=0)
    mine = lax.all_gather(near, "x", axis=0)
    x_size = mine.shape[0]
    yl_size = lax.axis_size("yl")
    mine = mine.reshape(x_size, 2, yl_size, cols, chans)

    sent = features.reshape(block, 3, sources, chans).transpose(2, 1, 0, 3)
    rows = lax.all_to_all(sent, CHAN, 0, 0, tiled=True)
    halo_blocks = -(-(KMR + KS - 1) // block)
    tail = jnp.concatenate(
        [rows[sources - halo_blocks :, 1:].reshape(2 * halo_blocks, block, chans), rows[sources - 1 :, 0]],
        axis=0,
    )
    shards = lax.axis_size(SEQ)
    halo = lax.ppermute(tail, SEQ, [(i, i + 1) for i in range(shards - 1)])

    groups = mr_filter.shape[0]
    band = call(
        bands_kernel,
        flops=groups * KMR * KMR * 4,
        moved=groups * 2 * KMR * KMR * 2,
        out_shape=jax.ShapeDtypeStruct((groups, 2 * KMR, KMR), bf16),
        in_specs=[vmem],
        out_specs=vmem,
    )(mr_filter)

    per_step = LANES // GROUP
    halo_rows = halo_blocks * block
    gated = call(
        conv_kernel,
        flops=tokens * chans * 256 * 2,
        moved=rows.size * 2 + halo.size * 2 + band.size * 2,
        grid=(chans // LANES,),
        out_shape=jax.ShapeDtypeStruct((tokens, chans), bf16),
        in_specs=[
            pl.BlockSpec((sources, 3, block, LANES), lambda i: (0, 0, 0, i)),
            pl.BlockSpec((2 * halo_blocks + 1, block, LANES), lambda i: (0, 0, i)),
            pl.BlockSpec((3, KS, LANES), lambda i: (0, 0, i)),
            pl.BlockSpec((per_step, 2 * KMR, KMR), lambda i: (i, 0, 0)),
        ],
        out_specs=pl.BlockSpec((tokens, LANES), lambda i: (0, i)),
        scratch_shapes=[
            pltpu.VMEM((block + tokens, LANES), f32),
            pltpu.VMEM((halo_rows + tokens, LANES), f32),
            pltpu.VMEM((halo_rows + tokens, LANES), f32),
            pltpu.VMEM((LANES, KMR + tokens), bf16),
            pltpu.VMEM((LANES, tokens), f32),
        ],
    )(rows, halo, short_taps.transpose(1, 0, 2), band)

    pair = lax.ppermute(gated, "par", [(0, 1), (1, 0)])
    mine, gated = lax.optimization_barrier((mine, gated))
    other = lax.ppermute(mine, "core", [(0, 1), (1, 0)])
    out_cols = 2 * yl_size * cols
    whole = pl.BlockSpec((tokens, chans), lambda i: (0, 0))
    slab = pl.BlockSpec((1, 2, yl_size, cols, chans), lambda i: (i, 0, 0, 0, 0))
    partial = call(
        project_kernel,
        flops=tokens * 2 * chans * x_size * out_cols * 2,
        moved=mine.size * 4 + x_size * tokens * out_cols * 2 + gated.size * 4,
        grid=(x_size,),
        out_shape=jax.ShapeDtypeStruct((x_size, tokens, out_cols), bf16),
        in_specs=[smem, whole, whole, slab, slab],
        out_specs=pl.BlockSpec((1, tokens, out_cols), lambda i: (i, 0, 0)),
        scratch_shapes=[pltpu.VMEM((2, tokens, chans), bf16)],
    )(lax.axis_index("par").reshape(1), gated, pair, mine, other)

    parts = lax.all_to_all(partial, ("Y", "zz"), 0, 0, tiled=True)
    return call(
        sum_kernel,
        flops=parts.size,
        moved=parts.size * 2 + residual.size * 4,
        out_shape=jax.ShapeDtypeStruct(residual.shape, residual.dtype),
        in_specs=[smem, vmem, vmem],
        out_specs=vmem,
    )(lax.axis_index("core").reshape(1), parts, residual)


def split(mesh, sizes):
    return Mesh(mesh.devices.reshape(sizes), SEQ + CHAN)


def solution(mesh):
    fine = split(mesh, (8, 2, 2, 2, 2, 4, 2))
    placed = (
        P(SEQ + CHAN, None, None),
        P(None, None, CHAN),
        P(CHAN, None),
        P(CHAN, SEQ),
        P(SEQ, CHAN),
    )
    return jax.shard_map(body, mesh=fine, in_specs=placed, out_specs=P(SEQ, CHAN), check_vma=False)
```

time: 407 us -> 164 us (0.40)
  the two profiles are of different devices: /device:TPU:2 before, /device:TPU:18 now
where the time goes in v1:
time: 164 us
  blocking collectives  66.9 us (41%)
  waiting for transfers between devices  51.1 us (31%)
  starting transfers between devices  21.3 us (13%)
  between operations  13.5 us (8%)
  Pallas kernels  8.02 us (5%)
  local copies, waits for them, and re-layouts  2.87 us (2%)
    all_to_all x1, blocking collectives, body(): rows = lax.all_to_all(sent, CHAN, 0, 0, tiled=True)  43.9 us
    all_to_all x1, waiting for transfers between devices, body(): parts = lax.all_to_all(partial, ('Y', 'zz'), 0, 0, tiled=True)  37.5 us
    all_gather x1, blocking collectives, body(): near = lax.all_gather(weight, ('yh', 'yl'), axis=0)  23 us
    all_to_all x1, starting transfers between devices, body(): parts = lax.all_to_all(partial, ('Y', 'zz'), 0, 0, tiled=True)  12.2 us
    ppermute x1, waiting for transfers between devices, body(): pair = lax.ppermute(gated, 'par', [(0, 1), (1, 0)])  6.95 us
    ppermute x1, waiting for transfers between devices, body(): halo = lax.ppermute(tail, SEQ, [(i, i + 1) for i in range(shards - 1)])  5.89 us
    pallas_call x1, Pallas kernels, body(): call(project_kernel, flops=tokens * 2 * chans * x_size * out_cols * 2, mo...  4.36 us
    ppermute x1, starting transfers between devices, body(): pair = lax.ppermute(gated, 'par', [(0, 1), (1, 0)])  3.74 us
  transfers between devices with their start and end apart: 6, of which 4 were waited for; matrix products, arithmetic and copies ran while one was open for 1% of the time, Pallas kernels for 2%

profile of v1, /device:TPU:18, one launch (start us, length us, event | category | flops | bytes accessed | tf_op | source)
XLA Modules:
  0.0 163.7 jit_solution(1805859768369803525)
XLA Ops:
  6.5 0.0 all-gather.4.cloned.1.call-start
  6.5 1.5 collective-permute-start
  8.0 0.0 collective-permute-done
  8.0 23.0 %all-gather = bf16[256,512]{1,0:T(8,128)(2,1)} all-gather(bf16[64,512]{1,0:T(8,128)(2,1)S(1)} %collective-permute-done), channel_id=2, replica_groups=mesh['x'=8,'yh'=2,'yl'=2,'core'=2,'Y'=2,'zz'=4,'par'=2] {'yh','yl'}, dimensions={0}, use_global_device_ids=true | all-gather | bytes 327680 | tf_op jit(solution)/shard_map/all_gather | solution.py:121
  31.0 0.0 all-gather.4.cloned.1.call-update
  31.1 0.0 copy-start.3
  31.1 1.2 copy.10
  32.3 0.0 copy-start.2
  32.3 43.9 %all_to_all.10.rows_ref = bf16[16,3,16,512]{3,2,1,0:T(8,128)(2,1)S(1)} all-to-all(bf16[16,3,16,512]{3,2,1,0:T(8,128)(2,1)S(1)} %bitcast.19), channel_id=1, replica_groups=mesh['x'=8,'yh'=2,'yl'=2,'core'=2,'Y'=2,'zz'=4,'par'=2] {'Y','zz','par'}, dimensions={0} | all-to-all | bytes 1572864 | tf_op jit(solution)/shard_map/all_to_all | solution.py:128
  76.3 1.9 %collective-permute-start.1 = (bf16[19,16,512]{2,1,0:T(8,128)(2,1)S(1)}, bf16[19,16,512]{2,1,0:T(8,128)(2,1)S(1)}, u32[]{:S(2)}, u32[]{:S(2)}) collective-permute-start(bf16[19,16,512]{2,1,0:T(8,128)(2,1)S(1)} %pad_maximum_fusion), channel_id=1, source_target_pairs={{0,16},{16,32},{32,48},{48,64},{64,80},{80,96},{96,112},{112,128},... | collective-permute-start | bytes 933896 | tf_op jit(solution)/shard_map/ppermute | solution.py:135
  78.3 0.0 copy-done.3
  78.3 0.4 shard_map.55.band_ref
  78.7 5.9 %collective-permute-done.1.halo_ref = bf16[19,16,512]{2,1,0:T(8,128)(2,1)S(1)} collective-permute-done((bf16[19,16,512]{2,1,0:T(8,128)(2,1)S(1)}, bf16[19,16,512]{2,1,0:T(8,128)(2,1)S(1)}, u32[]{:S(2)}, u32[]{:S(2)}) %collective-permute-start.1) | collective-permute-done | bytes 311328 | tf_op jit(solution)/shard_map/ppermute | solution.py:135
  84.5 0.0 copy-done.2
  84.6 2.4 %shard_map.56.own_ref = bf16[256,512]{1,0:T(8,128)(2,1)S(1)} custom-call(bf16[16,3,16,512]{3,2,1,0:T(8,128)(2,1)S(1)} %all_to_all.10.rows_ref, bf16[19,16,512]{2,1,0:T(8,128)(2,1)S(1)} %collective-permute-done.1.halo_ref, f32[3,7,512]{2,1,0:T(8,128)S(1)} %bitcast.18, bf16[32,256,128]{2,1,0:T(8,128)(2,1)S(1)} %shard_map.55.band_ref), custom_call_target="tpu_custom_call" | custom-call | flops 67108864 | bytes 3194880 | tf_op jit(solution)/shard_map/pallas_call | solution.py:149
  87.0 0.7 all-gather.4.cloned.1.call-done
  87.7 1.9 %collective-permute-start.3 = (bf16[8,2,2,64,512]{4,3,2,1,0:T(8,128)(2,1)}, bf16[8,2,2,64,512]{4,3,2,1,0:T(8,128)(2,1)S(1)}, u32[]{:S(2)}, u32[]{:S(2)}) collective-permute-start(bf16[8,2,2,64,512]{4,3,2,1,0:T(8,128)(2,1)} %bitcast.16), channel_id=1, source_target_pairs={{0,16},{16,0},{1,17},{17,1},{2,18},{18,2},{3,19},{19,3},{4,20},{20... | collective-permute-start | bytes 6291464 | tf_op jit(solution)/shard_map/ppermute | solution.py:173
  89.6 3.7 %collective-permute-start.2 = (bf16[256,512]{1,0:T(8,128)(2,1)S(1)}, bf16[256,512]{1,0:T(8,128)(2,1)S(1)}, u32[]{:S(2)}, u32[]{:S(2)}) collective-permute-start(bf16[256,512]{1,0:T(8,128)(2,1)S(1)} %shard_map.56.own_ref), channel_id=1, source_target_pairs={{0,1},{1,0},{2,3},{3,2},{4,5},{5,4},{6,7},{7,6},{8,9},{9,8},{10,11... | collective-permute-start | bytes 786440 | tf_op jit(solution)/shard_map/ppermute | solution.py:171
  93.4 6.9 %collective-permute-done.2.pair_ref = bf16[256,512]{1,0:T(8,128)(2,1)S(1)} collective-permute-done((bf16[256,512]{1,0:T(8,128)(2,1)S(1)}, bf16[256,512]{1,0:T(8,128)(2,1)S(1)}, u32[]{:S(2)}, u32[]{:S(2)}) %collective-permute-start.2) | collective-permute-done | bytes 262176 | tf_op jit(solution)/shard_map/ppermute | solution.py:171
  100.3 0.0 collective-permute-done.3.other_ref
  100.3 0.0 copy-start
  100.3 1.6 copy-done
  101.9 4.4 %shard_map.57 = bf16[8,256,256]{2,1,0:T(8,128)(2,1)} custom-call(s32[1]{0:T(128)} %bitcast.1.par_ref, bf16[256,512]{1,0:T(8,128)(2,1)S(1)} %shard_map.56.own_ref, bf16[256,512]{1,0:T(8,128)(2,1)S(1)} %collective-permute-done.2.pair_ref, bf16[8,2,2,64,512]{4,3,2,1,0:T(8,128)(2,1)S(1)} %bitcast.17, bf16[8,2,2,64,512]{4,3,2,1,0:T(8,128)(2,1)S(1)} %collective-permute-done.3.other_ref), custom_call_target="tpu_custom_call" | custom-call | flops 1073741824 | bytes 5767168 | tf_op jit(solution)/shard_map/pallas_call | solution.py:177
  106.3 0.0 copy-start.1
  106.3 12.2 %all-to-all-start.1 = ((bf16[8,256,256]{2,1,0:T(8,128)(2,1)}), bf16[8,256,256]{2,1,0:T(8,128)(2,1)S(1)}, u32[]{:S(2)}, u32[]{:S(2)}) async-start(bf16[8,256,256]{2,1,0:T(8,128)(2,1)} %shard_map.57), calls=%async_computation.1 | async-start | bytes 2097152 | tf_op jit(solution)/shard_map/all_to_all | solution.py:188
  118.5 37.5 %all-to-all-done.1.parts_ref = bf16[8,256,256]{2,1,0:T(8,128)(2,1)S(1)} async-done(((bf16[8,256,256]{2,1,0:T(8,128)(2,1)}), bf16[8,256,256]{2,1,0:T(8,128)(2,1)S(1)}, u32[]{:S(2)}, u32[]{:S(2)}) %all-to-all-start.1) | async-done | bytes 1048608 | tf_op jit(solution)/shard_map/all_to_all | solution.py:188
  156.0 0.0 copy-done.1
  156.0 0.9 shard_map.58
  (3 shorter events, 0.1 us)
Async XLA Ops:
  6.5 81.2 %all-gather.4.cloned.1.call-start = ((), (), s32[]{:S(2)}) async-start(), calls=%async_computation.2 | async-start | bytes 2359296 | tf_op jit(solution)/shard_map/all_gather | solution.py:122
  6.5 1.5 collective-permute-start
  31.1 47.2 %copy-start.3 = (f32[32,128]{1,0:T(8,128)S(1)}, f32[32,128]{1,0:T(8,128)}, u32[]{:S(2)}) copy-start(f32[32,128]{1,0:T(8,128)} %filter_ref.1) | copy-start | bytes 49156
  32.3 52.2 %copy-start.2 = (f32[7,3,512]{2,0,1:T(8,128)S(1)}, f32[7,3,512]{2,0,1:T(8,128)}, u32[]{:S(2)}) copy-start(f32[7,3,512]{2,0,1:T(8,128)} %param.6) | copy-start | bytes 129028
  76.3 8.2 %collective-permute-start.1 = (bf16[19,16,512]{2,1,0:T(8,128)(2,1)S(1)}, bf16[19,16,512]{2,1,0:T(8,128)(2,1)S(1)}, u32[]{:S(2)}, u32[]{:S(2)}) collective-permute-start(bf16[19,16,512]{2,1,0:T(8,128)(2,1)S(1)} %pad_maximum_fusion), channel_id=1, source_target_pairs={{0,16},{16,32},{32,48},{48,64},{64,80},{80,96},{96,112},{112,128},... | collective-permute-start | bytes 933896 | tf_op jit(solution)/shard_map/ppermute | solution.py:135
  87.7 12.6 %collective-permute-start.3 = (bf16[8,2,2,64,512]{4,3,2,1,0:T(8,128)(2,1)}, bf16[8,2,2,64,512]{4,3,2,1,0:T(8,128)(2,1)S(1)}, u32[]{:S(2)}, u32[]{:S(2)}) collective-permute-start(bf16[8,2,2,64,512]{4,3,2,1,0:T(8,128)(2,1)} %bitcast.16), channel_id=1, source_target_pairs={{0,16},{16,0},{1,17},{17,1},{2,18},{18,2},{3,19},{19,3},{4,20},{20... | collective-permute-start | bytes 6291464 | tf_op jit(solution)/shard_map/ppermute | solution.py:173
  89.6 10.7 %collective-permute-start.2 = (bf16[256,512]{1,0:T(8,128)(2,1)S(1)}, bf16[256,512]{1,0:T(8,128)(2,1)S(1)}, u32[]{:S(2)}, u32[]{:S(2)}) collective-permute-start(bf16[256,512]{1,0:T(8,128)(2,1)S(1)} %shard_map.56.own_ref), channel_id=1, source_target_pairs={{0,1},{1,0},{2,3},{3,2},{4,5},{5,4},{6,7},{7,6},{8,9},{9,8},{10,11... | collective-permute-start | bytes 786440 | tf_op jit(solution)/shard_map/ppermute | solution.py:171
  100.3 1.6 copy-start
  106.3 49.7 %copy-start.1 = (bf16[256,256]{1,0:T(8,128)(2,1)S(1)}, bf16[256,256]{1,0:T(8,128)(2,1)}, u32[]{:S(2)}) copy-start(bf16[256,256]{1,0:T(8,128)(2,1)} %residual_ref.1) | copy-start | bytes 393220
  106.3 49.7 %all-to-all-start.1 = ((bf16[8,256,256]{2,1,0:T(8,128)(2,1)}), bf16[8,256,256]{2,1,0:T(8,128)(2,1)S(1)}, u32[]{:S(2)}, u32[]{:S(2)}) async-start(bf16[8,256,256]{2,1,0:T(8,128)(2,1)} %shard_map.57), calls=%async_computation.1 | async-start | bytes 2097152 | tf_op jit(solution)/shard_map/all_to_all | solution.py:188
Sparse Core Ops, SparseCore 0:
  31.2 56.4 all-gather.3

commit v2 on v1

--- a/solution.py
+++ b/solution.py
@@ -5,6 +5,7 @@
 from jax.experimental.pallas import tpu as pltpu
 from jax.sharding import Mesh
 from jax.sharding import PartitionSpec as P
+
 
 KS = 7
 KMR = 128
@@ -69,42 +70,49 @@
         for i in range(spans):
             mixed_t[chans, i * KMR : (i + 1) * KMR] = out[i * GROUP : (i + 1) * GROUP]
     for i in range(spans):
-        query = short_rows(q_ext, taps_q, block + i * KMR, KMR)
-        mixed = mixed_t[:, i * KMR : (i + 1) * KMR].T
-        gated_ref[i * KMR : (i + 1) * KMR, :] = (query * mixed).astype(gated_ref.dtype)
-
-
-def project_kernel(par_ref, own_ref, pair_ref, mine_ref, other_ref, out_ref, both):
+        query = short_rows(q_ext, taps_q, block + i * KMR, KMR).T
+        mixed = mixed_t[:, i * KMR : (i + 1) * KMR]
+        gated_ref[:, i * KMR : (i + 1) * KMR] = (query * mixed).astype(gated_ref.dtype)
+
+
+def project_kernel(place_ref, own_ref, pair_ref, weight_ref, out_ref, both):
     @pl.when(pl.program_id(0) == 0)
     def _():
-        par = par_ref[0]
-        both[par] = own_ref[...]
-        both[1 - par] = pair_ref[...]
-
-    total = None
-    for b in range(2):
-        pieces = []
-        for yl in range(mine_ref.shape[2]):
-            pieces += [mine_ref[0, b, yl], other_ref[0, b, yl]]
-        term = lax.dot_general(
-            both[b],
-            jnp.concatenate(pieces, axis=0),
-            (((1,), (1,)), ((), ())),
-            preferred_element_type=jnp.float32,
-        )
-        total = term if total is None else total + term
-    out_ref[0] = total.astype(out_ref.dtype)
-
-
-def sum_kernel(core_ref, parts_ref, residual_ref, out_ref):
+        slot = place_ref[0]
+        both[slot] = own_ref[...]
+        both[1 - slot] = pair_ref[...]
+
+    steps, cores, _, yl_size, _, _ = weight_ref.shape
+    for step in range(steps):
+        total = None
+        for slot in range(2):
+            pieces = [weight_ref[step, core, slot, yl] for yl in range(yl_size) for core in range(cores)]
+            term = jnp.dot(
+                jnp.concatenate(pieces, axis=0), both[slot], preferred_element_type=jnp.float32
+            )
+            total = term if total is None else total + term
+        out_ref[step] = total.astype(out_ref.dtype)
+
+
+def sum_kernel(place_ref, parts_ref, residual_ref, out_ref):
     total = parts_ref[0].astype(jnp.float32)
     for i in range(1, parts_ref.shape[0]):
         total = total + parts_ref[i].astype(jnp.float32)
-    for i in range(total.shape[1] // LANES):
-        lanes = slice(i * LANES, (i + 1) * LANES)
-        piece = total[:, lanes]
-        piece = jnp.where(core_ref[0] == 0, piece, pltpu.roll(piece, LANES // 2, 1))
+    half = total.shape[0] // 2
+    first, second = total[:half], total[half:]
+    for i, (piece, swapped) in enumerate(((first, second), (second, first))):
+        lanes = slice(i * half, (i + 1) * half)
+        piece = jnp.where(place_ref[0] == 0, piece, swapped).T
         out_ref[:, lanes] = (residual_ref[:, lanes].astype(jnp.float32) + piece).astype(out_ref.dtype)
+
+
+def weight_route(pair_step, yl_step):
+    return [
+        ((yh * 2 + yl) * 2 + par, ((par ^ pair_step) * 2 + (yl ^ yl_step)) * 2 + yh)
+        for yh in range(2)
+        for yl in range(2)
+        for par in range(2)
+    ]
 
 
 def body(features, short_taps, mr_filter, out_weight, residual):
@@ -116,13 +124,16 @@
     vmem = pl.BlockSpec(memory_space=pltpu.VMEM)
     smem = pl.BlockSpec(memory_space=pltpu.SMEM)
 
-    weight = lax.ppermute(out_weight.T, ("yh", "par"), [(0, 0), (1, 2), (2, 1), (3, 3)])
-    cols = weight.shape[0]
-    near = lax.all_gather(weight, ("yh", "yl"), axis=0)
-    mine = lax.all_gather(near, "x", axis=0)
-    x_size = mine.shape[0]
-    yl_size = lax.axis_size("yl")
-    mine = mine.reshape(x_size, 2, yl_size, cols, chans)
+    near = [
+        lax.ppermute(out_weight.T, ("yh", "yl", "par"), weight_route(pair_step, yl_step))
+        for pair_step in range(2)
+        for yl_step in range(2)
+    ]
+    cols = near[0].shape[0]
+    near = jnp.stack(near).reshape(2, 2, cols, chans)
+    whole_weight = lax.all_gather(near, ("x", "core"), axis=0)
+    x_size = lax.axis_size("x")
+    whole_weight = whole_weight.reshape(x_size, -1, *near.shape)
 
     sent = features.reshape(block, 3, sources, chans).transpose(2, 1, 0, 3)
     rows = lax.all_to_all(sent, CHAN, 0, 0, tiled=True)
@@ -151,14 +162,14 @@
         flops=tokens * chans * 256 * 2,
         moved=rows.size * 2 + halo.size * 2 + band.size * 2,
         grid=(chans // LANES,),
-        out_shape=jax.ShapeDtypeStruct((tokens, chans), bf16),
+        out_shape=jax.ShapeDtypeStruct((chans, tokens), bf16),
         in_specs=[
             pl.BlockSpec((sources, 3, block, LANES), lambda i: (0, 0, 0, i)),
             pl.BlockSpec((2 * halo_blocks + 1, block, LANES), lambda i: (0, 0, i)),
             pl.BlockSpec((3, KS, LANES), lambda i: (0, 0, i)),
             pl.BlockSpec((per_step, 2 * KMR, KMR), lambda i: (i, 0, 0)),
         ],
-        out_specs=pl.BlockSpec((tokens, LANES), lambda i: (0, i)),
+        out_specs=pl.BlockSpec((LANES, tokens), lambda i: (i, 0)),
         scratch_shapes=[
             pltpu.VMEM((block + tokens, LANES), f32),
             pltpu.VMEM((halo_rows + tokens, LANES), f32),
@@ -169,21 +180,26 @@
     )(rows, halo, short_taps.transpose(1, 0, 2), band)
 
     pair = lax.ppermute(gated, "par", [(0, 1), (1, 0)])
-    mine, gated = lax.optimization_barrier((mine, gated))
-    other = lax.ppermute(mine, "core", [(0, 1), (1, 0)])
-    out_cols = 2 * yl_size * cols
-    whole = pl.BlockSpec((tokens, chans), lambda i: (0, 0))
-    slab = pl.BlockSpec((1, 2, yl_size, cols, chans), lambda i: (i, 0, 0, 0, 0))
+    whole_weight, pair = lax.optimization_barrier((whole_weight, pair))
+    out_cols = whole_weight.size // (x_size * 2 * chans)
+    both = pl.BlockSpec((chans, tokens), lambda i: (0, 0))
+    per_call = 2
     partial = call(
         project_kernel,
+        vmem_mib=20,
         flops=tokens * 2 * chans * x_size * out_cols * 2,
-        moved=mine.size * 4 + x_size * tokens * out_cols * 2 + gated.size * 4,
-        grid=(x_size,),
-        out_shape=jax.ShapeDtypeStruct((x_size, tokens, out_cols), bf16),
-        in_specs=[smem, whole, whole, slab, slab],
-        out_specs=pl.BlockSpec((1, tokens, out_cols), lambda i: (i, 0, 0)),
-        scratch_shapes=[pltpu.VMEM((2, tokens, chans), bf16)],
-    )(lax.axis_index("par").reshape(1), gated, pair, mine, other)
+        moved=whole_weight.size * 2 + x_size * tokens * out_cols * 2 + gated.size * 4,
+        grid=(x_size // per_call,),
+        out_shape=jax.ShapeDtypeStruct((x_size, out_cols, tokens), bf16),
+        in_specs=[
+            smem,
+            both,
+            both,
+            pl.BlockSpec((per_call, *whole_weight.shape[1:]), lambda i: (i, 0, 0, 0, 0, 0)),
+        ],
+        out_specs=pl.BlockSpec((per_call, out_cols, tokens), lambda i: (i, 0, 0)),
+        scratch_shapes=[pltpu.VMEM((2, chans, tokens), bf16)],
+    )((lax.axis_index("par") ^ lax.axis_index("yh")).reshape(1), gated, pair, whole_weight)
 
     parts = lax.all_to_all(partial, ("Y", "zz"), 0, 0, tiled=True)
     return call(
@@ -193,7 +209,7 @@
         out_shape=jax.ShapeDtypeStruct(residual.shape, residual.dtype),
         in_specs=[smem, vmem, vmem],
         out_specs=vmem,
-    )(lax.axis_index("core").reshape(1), parts, residual)
+    )(lax.axis_index("yl").reshape(1), parts, residual)
 
 
 def split(mesh, sizes):

time: 164 us -> 149 us (0.909)
  the two profiles are of different devices: /device:TPU:18 before, /device:TPU:94 now
where the time goes in v2:
time: 149 us; the launch traced here: 148 us
  waiting for transfers between devices  52.9 us (36%)
  blocking collectives  44.8 us (30%)
  starting transfers between devices  26.6 us (18%)
  between operations  13.5 us (9%)
  Pallas kernels  6.2 us (4%)
  local copies, waits for them, and re-layouts  3.45 us (2%)
    all_to_all x1, blocking collectives, body(): rows = lax.all_to_all(sent, CHAN, 0, 0, tiled=True)  44.8 us
    all_to_all x1, waiting for transfers between devices, body(): parts = lax.all_to_all(partial, ('Y', 'zz'), 0, 0, tiled=True)  38.7 us
    ppermute x4, starting transfers between devices, body(): lax.ppermute(out_weight.T, ('yh', 'yl', 'par'), weight_route(pair_step, y...  13.1 us
    all_to_all x1, starting transfers between devices, body(): parts = lax.all_to_all(partial, ('Y', 'zz'), 0, 0, tiled=True)  8.68 us
    ppermute x1, waiting for transfers between devices, body(): pair = lax.ppermute(gated, 'par', [(0, 1), (1, 0)])  6.13 us
    ppermute x1, waiting for transfers between devices, body(): halo = lax.ppermute(tail, SEQ, [(i, i + 1) for i in range(shards - 1)])  5.89 us
  transfers between devices with their start and end apart: 8, of which 4 were waited for; matrix products, arithmetic and copies ran while one was open for 1% of the time, Pallas kernels for 2%

profile of v2, /device:TPU:94, one launch (start us, length us, event | category | flops | bytes accessed | tf_op | source)
XLA Modules:
  0.0 148.2 jit_solution(801954255981655258)
XLA Ops:
  6.5 0.0 copy-start.3
  6.5 0.0 copy-start.2
  6.5 0.0 all-gather.2.cloned.1.call-start
  6.5 2.8 %collective-permute-start.4 = (bf16[64,512]{1,0:T(8,128)(2,1)}, bf16[64,512]{1,0:T(8,128)(2,1)S(1)}, u32[]{:S(2)}, u32[]{:S(2)}) collective-permute-start(bf16[64,512]{1,0:T(8,128)(2,1)} %bitcast.30), channel_id=1, source_target_pairs={{0,96},{1,32},{32,64},{33,0},{64,97},{65,33},{96,65},{97,1},{2,98}... | collective-permute-start | bytes 196616 | tf_op jit(solution)/shard_map/ppermute | solution.py:128
  9.4 6.1 %collective-permute-start.3 = (bf16[64,512]{1,0:T(8,128)(2,1)}, bf16[64,512]{1,0:T(8,128)(2,1)S(1)}, u32[]{:S(2)}, u32[]{:S(2)}) collective-permute-start(bf16[64,512]{1,0:T(8,128)(2,1)} %bitcast.31), channel_id=1, source_target_pairs={{0,64},{1,0},{32,96},{33,32},{64,65},{65,1},{96,97},{97,33},{2,66}... | collective-permute-start | bytes 196616 | tf_op jit(solution)/shard_map/ppermute | solution.py:128
  15.5 2.7 %collective-permute-start.2 = (bf16[64,512]{1,0:T(8,128)(2,1)}, bf16[64,512]{1,0:T(8,128)(2,1)S(1)}, u32[]{:S(2)}, u32[]{:S(2)}) collective-permute-start(bf16[64,512]{1,0:T(8,128)(2,1)} %bitcast.32), channel_id=1, source_target_pairs={{0,32},{1,96},{32,0},{33,64},{64,33},{65,97},{96,1},{97,65},{2,34}... | collective-permute-start | bytes 196616 | tf_op jit(solution)/shard_map/ppermute | solution.py:128
  18.2 1.5 %collective-permute-start.1 = (bf16[64,512]{1,0:T(8,128)(2,1)}, bf16[64,512]{1,0:T(8,128)(2,1)S(1)}, u32[]{:S(2)}, u32[]{:S(2)}) collective-permute-start(bf16[64,512]{1,0:T(8,128)(2,1)} %bitcast.33), channel_id=1, source_target_pairs={{0,0},{1,64},{32,32},{33,96},{64,1},{65,65},{96,33},{97,97},{2,2},... | collective-permute-start | bytes 196616 | tf_op jit(solution)/shard_map/ppermute | solution.py:128
  19.7 0.0 collective-permute-done.4
  19.7 0.0 collective-permute-done.3
  19.7 2.2 %collective-permute-done.2 = bf16[64,512]{1,0:T(8,128)(2,1)S(1)} collective-permute-done((bf16[64,512]{1,0:T(8,128)(2,1)}, bf16[64,512]{1,0:T(8,128)(2,1)S(1)}, u32[]{:S(2)}, u32[]{:S(2)}) %collective-permute-start.2) | collective-permute-done | bytes 65568 | tf_op jit(solution)/shard_map/ppermute | solution.py:128
  21.8 0.0 collective-permute-done.1
  21.8 0.7 pad_maximum_fusion.1
  22.6 0.0 all-gather.2.cloned.1.call-update
  22.6 1.2 copy.10
  23.8 44.8 %all_to_all.10.rows_ref = bf16[16,3,16,512]{3,2,1,0:T(8,128)(2,1)S(1)} all-to-all(bf16[16,3,16,512]{3,2,1,0:T(8,128)(2,1)S(1)} %bitcast.22), channel_id=1, replica_groups=mesh['x'=8,'yh'=2,'yl'=2,'core'=2,'Y'=2,'zz'=4,'par'=2] {'Y','zz','par'}, dimensions={0} | all-to-all | bytes 1572864 | tf_op jit(solution)/shard_map/all_to_all | solution.py:139
  68.7 1.9 %collective-permute-start = (bf16[19,16,512]{2,1,0:T(8,128)(2,1)S(1)}, bf16[19,16,512]{2,1,0:T(8,128)(2,1)S(1)}, u32[]{:S(2)}, u32[]{:S(2)}) collective-permute-start(bf16[19,16,512]{2,1,0:T(8,128)(2,1)S(1)} %pad_maximum_fusion), channel_id=1, source_target_pairs={{0,16},{16,32},{32,48},{48,64},{64,80},{80,96},{96,112},{112,128},... | collective-permute-start | bytes 933896 | tf_op jit(solution)/shard_map/ppermute | solution.py:146
  70.6 0.0 copy-done.3
  70.6 0.4 shard_map.55.band_ref
  71.0 5.9 %collective-permute-done.halo_ref = bf16[19,16,512]{2,1,0:T(8,128)(2,1)S(1)} collective-permute-done((bf16[19,16,512]{2,1,0:T(8,128)(2,1)S(1)}, bf16[19,16,512]{2,1,0:T(8,128)(2,1)S(1)}, u32[]{:S(2)}, u32[]{:S(2)}) %collective-permute-start) | collective-permute-done | bytes 311328 | tf_op jit(solution)/shard_map/ppermute | solution.py:146
  76.9 0.0 copy-done.2
  76.9 0.0 copy-start.1
  76.9 2.1 %shard_map.56.own_ref = bf16[512,256]{1,0:T(8,128)(2,1)S(1)} custom-call(bf16[16,3,16,512]{3,2,1,0:T(8,128)(2,1)S(1)} %all_to_all.10.rows_ref, bf16[19,16,512]{2,1,0:T(8,128)(2,1)S(1)} %collective-permute-done.halo_ref, f32[3,7,512]{2,1,0:T(8,128)S(1)} %bitcast.21, bf16[32,256,128]{2,1,0:T(8,128)(2,1)S(1)} %shard_map.55.band_ref), custom_call_target="tpu_custom_call" | custom-call | flops 67108864 | bytes 3194880 | tf_op jit(solution)/shard_map/pallas_call | solution.py:160
  79.1 2.9 %collective-permute-start.5 = (bf16[512,256]{1,0:T(8,128)(2,1)S(1)}, bf16[512,256]{1,0:T(8,128)(2,1)S(1)}, u32[]{:S(2)}, u32[]{:S(2)}) collective-permute-start(bf16[512,256]{1,0:T(8,128)(2,1)S(1)} %shard_map.56.own_ref), channel_id=1, source_target_pairs={{0,1},{1,0},{2,3},{3,2},{4,5},{5,4},{6,7},{7,6},{8,9},{9,8},{10,11... | collective-permute-start | bytes 786440 | tf_op jit(solution)/shard_map/ppermute | solution.py:182
  82.0 6.1 %collective-permute-done.5.pair_ref = bf16[512,256]{1,0:T(8,128)(2,1)S(1)} collective-permute-done((bf16[512,256]{1,0:T(8,128)(2,1)S(1)}, bf16[512,256]{1,0:T(8,128)(2,1)S(1)}, u32[]{:S(2)}, u32[]{:S(2)}) %collective-permute-start.5) | collective-permute-done | bytes 262176 | tf_op jit(solution)/shard_map/ppermute | solution.py:182
  88.1 0.0 all-gather.2.cloned.1.call-done
  88.1 0.0 copy-start
  88.1 2.2 %copy-done = bf16[16,2,2,64,512]{4,3,2,1,0:T(8,128)(2,1)S(1)} copy-done((bf16[16,2,2,64,512]{4,3,2,1,0:T(8,128)(2,1)S(1)}, bf16[16,2,2,64,512]{4,3,2,1,0:T(8,128)(2,1)}, u32[]{:S(2)}) %copy-start) | copy-done | bytes 4194328
  90.3 2.8 %shard_map.57 = bf16[8,256,256]{2,1,0:T(8,128)(2,1)} custom-call(s32[1]{0:T(128)} %bitcast.1.place_ref, bf16[512,256]{1,0:T(8,128)(2,1)S(1)} %shard_map.56.own_ref, bf16[512,256]{1,0:T(8,128)(2,1)S(1)} %collective-permute-done.5.pair_ref, bf16[8,2,2,2,64,512]{5,4,3,2,1,0:T(8,128)(2,1)S(1)} %bitcast.20), custom_call_target="tpu_custom_call" | custom-call | flops 1073741824 | bytes 5767168 | tf_op jit(solution)/shard_map/pallas_call | solution.py:187
  93.1 8.7 %all-to-all-start.1 = ((bf16[8,256,256]{2,1,0:T(8,128)(2,1)}), bf16[8,256,256]{2,1,0:T(8,128)(2,1)S(1)}, u32[]{:S(2)}, u32[]{:S(2)}) async-start(bf16[8,256,256]{2,1,0:T(8,128)(2,1)} %shard_map.57), calls=%async_computation.1 | async-start | bytes 2097152 | tf_op jit(solution)/shard_map/all_to_all | solution.py:204
  101.8 38.7 %all-to-all-done.1.parts_ref = bf16[8,256,256]{2,1,0:T(8,128)(2,1)S(1)} async-done(((bf16[8,256,256]{2,1,0:T(8,128)(2,1)}), bf16[8,256,256]{2,1,0:T(8,128)(2,1)S(1)}, u32[]{:S(2)}, u32[]{:S(2)}) %all-to-all-start.1) | async-done | bytes 1048608 | tf_op jit(solution)/shard_map/all_to_all | solution.py:204
  140.4 0.0 copy-done.1
  140.4 0.9 shard_map.58
  (3 shorter events, 0.1 us)
Async XLA Ops:
  6.5 64.1 %copy-start.3 = (f32[32,128]{1,0:T(8,128)S(1)}, f32[32,128]{1,0:T(8,128)}, u32[]{:S(2)}) copy-start(f32[32,128]{1,0:T(8,128)} %filter_ref.1) | copy-start | bytes 49156
  6.5 70.4 %copy-start.2 = (f32[7,3,512]{2,0,1:T(8,128)S(1)}, f32[7,3,512]{2,0,1:T(8,128)}, u32[]{:S(2)}) copy-start(f32[7,3,512]{2,0,1:T(8,128)} %param.6) | copy-start | bytes 129028
  6.5 81.6 %all-gather.2.cloned.1.call-start = ((), (), s32[]{:S(2)}) async-start(), calls=%async_computation.2 | async-start | bytes 4456448 | tf_op jit(solution)/shard_map/all_gather | solution.py:134
  6.5 13.1 %collective-permute-start.4 = (bf16[64,512]{1,0:T(8,128)(2,1)}, bf16[64,512]{1,0:T(8,128)(2,1)S(1)}, u32[]{:S(2)}, u32[]{:S(2)}) collective-permute-start(bf16[64,512]{1,0:T(8,128)(2,1)} %bitcast.30), channel_id=1, source_target_pairs={{0,96},{1,32},{32,64},{33,0},{64,97},{65,33},{96,65},{97,1},{2,98}... | collective-permute-start | bytes 196616 | tf_op jit(solution)/shard_map/ppermute | solution.py:128
  9.4 10.3 %collective-permute-start.3 = (bf16[64,512]{1,0:T(8,128)(2,1)}, bf16[64,512]{1,0:T(8,128)(2,1)S(1)}, u32[]{:S(2)}, u32[]{:S(2)}) collective-permute-start(bf16[64,512]{1,0:T(8,128)(2,1)} %bitcast.31), channel_id=1, source_target_pairs={{0,64},{1,0},{32,96},{33,32},{64,65},{65,1},{96,97},{97,33},{2,66}... | collective-permute-start | bytes 196616 | tf_op jit(solution)/shard_map/ppermute | solution.py:128
  15.5 6.4 %collective-permute-start.2 = (bf16[64,512]{1,0:T(8,128)(2,1)}, bf16[64,512]{1,0:T(8,128)(2,1)S(1)}, u32[]{:S(2)}, u32[]{:S(2)}) collective-permute-start(bf16[64,512]{1,0:T(8,128)(2,1)} %bitcast.32), channel_id=1, source_target_pairs={{0,32},{1,96},{32,0},{33,64},{64,33},{65,97},{96,1},{97,65},{2,34}... | collective-permute-start | bytes 196616 | tf_op jit(solution)/shard_map/ppermute | solution.py:128
  18.2 3.7 %collective-permute-start.1 = (bf16[64,512]{1,0:T(8,128)(2,1)}, bf16[64,512]{1,0:T(8,128)(2,1)S(1)}, u32[]{:S(2)}, u32[]{:S(2)}) collective-permute-start(bf16[64,512]{1,0:T(8,128)(2,1)} %bitcast.33), channel_id=1, source_target_pairs={{0,0},{1,64},{32,32},{33,96},{64,1},{65,65},{96,33},{97,97},{2,2},... | collective-permute-start | bytes 196616 | tf_op jit(solution)/shard_map/ppermute | solution.py:128
  68.7 8.2 %collective-permute-start = (bf16[19,16,512]{2,1,0:T(8,128)(2,1)S(1)}, bf16[19,16,512]{2,1,0:T(8,128)(2,1)S(1)}, u32[]{:S(2)}, u32[]{:S(2)}) collective-permute-start(bf16[19,16,512]{2,1,0:T(8,128)(2,1)S(1)} %pad_maximum_fusion), channel_id=1, source_target_pairs={{0,16},{16,32},{32,48},{48,64},{64,80},{80,96},{96,112},{112,128},... | collective-permute-start | bytes 933896 | tf_op jit(solution)/shard_map/ppermute | solution.py:146
  76.9 63.5 %copy-start.1 = (bf16[256,256]{1,0:T(8,128)(2,1)S(1)}, bf16[256,256]{1,0:T(8,128)(2,1)}, u32[]{:S(2)}) copy-start(bf16[256,256]{1,0:T(8,128)(2,1)} %residual_ref.1) | copy-start | bytes 393220
  79.1 9.0 %collective-permute-start.5 = (bf16[512,256]{1,0:T(8,128)(2,1)S(1)}, bf16[512,256]{1,0:T(8,128)(2,1)S(1)}, u32[]{:S(2)}, u32[]{:S(2)}) collective-permute-start(bf16[512,256]{1,0:T(8,128)(2,1)S(1)} %shard_map.56.own_ref), channel_id=1, source_target_pairs={{0,1},{1,0},{2,3},{3,2},{4,5},{5,4},{6,7},{7,6},{8,9},{9,8},{10,11... | collective-permute-start | bytes 786440 | tf_op jit(solution)/shard_map/ppermute | solution.py:182
  88.1 2.2 %copy-start = (bf16[16,2,2,64,512]{4,3,2,1,0:T(8,128)(2,1)S(1)}, bf16[16,2,2,64,512]{4,3,2,1,0:T(8,128)(2,1)}, u32[]{:S(2)}) copy-start(bf16[16,2,2,64,512]{4,3,2,1,0:T(8,128)(2,1)} %all-gather.2.cloned.1.call-done) | copy-start | bytes 12582916
  93.1 47.3 %all-to-all-start.1 = ((bf16[8,256,256]{2,1,0:T(8,128)(2,1)}), bf16[8,256,256]{2,1,0:T(8,128)(2,1)S(1)}, u32[]{:S(2)}, u32[]{:S(2)}) async-start(bf16[8,256,256]{2,1,0:T(8,128)(2,1)} %shard_map.57), calls=%async_computation.1 | async-start | bytes 2097152 | tf_op jit(solution)/shard_map/all_to_all | solution.py:204
Sparse Core Ops, SparseCore 0:
  22.7 60.5 all-gather.1

commit v3 on v2

--- a/solution.py
+++ b/solution.py
@@ -94,6 +94,17 @@
         out_ref[step] = total.astype(out_ref.dtype)
 
 
+def prefetch_kernel(weight_ref, out_ref, arrived):
+    copies = [
+        pltpu.make_async_copy(weight_ref.at[i], out_ref.at[i], arrived.at[i])
+        for i in range(out_ref.shape[0])
+    ]
+    for copy in copies:
+        copy.start()
+    for copy in copies:
+        copy.wait()
+
+
 def sum_kernel(place_ref, parts_ref, residual_ref, out_ref):
     total = parts_ref[0].astype(jnp.float32)
     for i in range(1, parts_ref.shape[0]):
@@ -124,11 +135,12 @@
     vmem = pl.BlockSpec(memory_space=pltpu.VMEM)
     smem = pl.BlockSpec(memory_space=pltpu.SMEM)
 
-    near = [
-        lax.ppermute(out_weight.T, ("yh", "yl", "par"), weight_route(pair_step, yl_step))
-        for pair_step in range(2)
-        for yl_step in range(2)
-    ]
+    near = []
+    for pair_step in range(2):
+        for yl_step in range(2):
+            near.append(
+                lax.ppermute(out_weight.T, ("yh", "yl", "par"), weight_route(pair_step, yl_step))
+            )
     cols = near[0].shape[0]
     near = jnp.stack(near).reshape(2, 2, cols, chans)
     whole_weight = lax.all_gather(near, ("x", "core"), axis=0)
@@ -180,7 +192,17 @@
     )(rows, halo, short_taps.transpose(1, 0, 2), band)
 
     pair = lax.ppermute(gated, "par", [(0, 1), (1, 0)])
-    whole_weight, pair = lax.optimization_barrier((whole_weight, pair))
+    whole_weight, gated = lax.optimization_barrier((whole_weight, gated))
+    whole_weight = pltpu.with_memory_space_constraint(whole_weight, pltpu.HBM)
+    whole_weight = call(
+        prefetch_kernel,
+        vmem_mib=20,
+        moved=whole_weight.size * 4,
+        out_shape=jax.ShapeDtypeStruct(whole_weight.shape, bf16),
+        in_specs=[pl.BlockSpec(memory_space=pltpu.HBM)],
+        out_specs=vmem,
+        scratch_shapes=[pltpu.SemaphoreType.DMA((x_size,))],
+    )(whole_weight)
     out_cols = whole_weight.size // (x_size * 2 * chans)
     both = pl.BlockSpec((chans, tokens), lambda i: (0, 0))
     per_call = 2

time: 149 us -> 150 us (level)
  the two profiles are of different devices: /device:TPU:94 before, /device:TPU:52 now
where the time goes in v3:
time: 150 us
  waiting for transfers between devices  58.6 us (39%)
  blocking collectives  41 us (27%)
  starting transfers between devices  26.2 us (17%)
  between operations  13.5 us (9%)
  Pallas kernels  8.41 us (6%)
    all_to_all x1, waiting for transfers between devices, body(): parts = lax.all_to_all(partial, ('Y', 'zz'), 0, 0, tiled=True)  42.8 us
    all_to_all x1, blocking collectives, body(): rows = lax.all_to_all(sent, CHAN, 0, 0, tiled=True)  41 us
    ppermute x4, starting transfers between devices, body(): lax.ppermute(out_weight.T, ('yh', 'yl', 'par'), weight_route(pair_step, y...  15.9 us
    ppermute x1, waiting for transfers between devices, body(): halo = lax.ppermute(tail, SEQ, [(i, i + 1) for i in range(shards - 1)])  8.05 us
    ppermute x1, waiting for transfers between devices, body(): pair = lax.ppermute(gated, 'par', [(0, 1), (1, 0)])  5.55 us
    all_to_all x1, starting transfers between devices, body(): parts = lax.all_to_all(partial, ('Y', 'zz'), 0, 0, tiled=True)  5.33 us
    ppermute x1, starting transfers between devices, body(): pair = lax.ppermute(gated, 'par', [(0, 1), (1, 0)])  3.04 us
  transfers between devices with their start and end apart: 8, of which 5 were waited for; matrix products, arithmetic and copies ran while one was open for 1% of the time, Pallas kernels for 3%

profile of v3, /device:TPU:52, one launch (start us, length us, event | category | flops | bytes accessed | tf_op | source)
XLA Modules:
  0.0 149.8 jit_solution(13720580484050279888)
XLA Ops:
  6.5 0.0 copy-start.2
  6.5 0.0 copy-start.1
  6.5 0.0 all-gather.2.cloned.1.call-start
  6.5 4.9 %collective-permute-start = (bf16[64,512]{1,0:T(8,128)(2,1)}, bf16[64,512]{1,0:T(8,128)(2,1)S(1)}, u32[]{:S(2)}, u32[]{:S(2)}) collective-permute-start(bf16[64,512]{1,0:T(8,128)(2,1)} %bitcast.30), channel_id=1, source_target_pairs={{0,0},{1,64},{32,32},{33,96},{64,1},{65,65},{96,33},{97,97},{2,2},... | collective-permute-start | bytes 196616 | tf_op jit(solution)/shard_map/ppermute | solution.py:142
  11.4 2.7 %collective-permute-start.1 = (bf16[64,512]{1,0:T(8,128)(2,1)}, bf16[64,512]{1,0:T(8,128)(2,1)S(1)}, u32[]{:S(2)}, u32[]{:S(2)}) collective-permute-start(bf16[64,512]{1,0:T(8,128)(2,1)} %bitcast.31), channel_id=1, source_target_pairs={{0,32},{1,96},{32,0},{33,64},{64,33},{65,97},{96,1},{97,65},{2,34}... | collective-permute-start | bytes 196616 | tf_op jit(solution)/shard_map/ppermute | solution.py:142
  14.1 1.9 %collective-permute-start.2 = (bf16[64,512]{1,0:T(8,128)(2,1)}, bf16[64,512]{1,0:T(8,128)(2,1)S(1)}, u32[]{:S(2)}, u32[]{:S(2)}) collective-permute-start(bf16[64,512]{1,0:T(8,128)(2,1)} %bitcast.32), channel_id=1, source_target_pairs={{0,64},{1,0},{32,96},{33,32},{64,65},{65,1},{96,97},{97,33},{2,66}... | collective-permute-start | bytes 196616 | tf_op jit(solution)/shard_map/ppermute | solution.py:142
  16.0 6.4 %collective-permute-start.3 = (bf16[64,512]{1,0:T(8,128)(2,1)}, bf16[64,512]{1,0:T(8,128)(2,1)S(1)}, u32[]{:S(2)}, u32[]{:S(2)}) collective-permute-start(bf16[64,512]{1,0:T(8,128)(2,1)} %bitcast.33), channel_id=1, source_target_pairs={{0,96},{1,32},{32,64},{33,0},{64,97},{65,33},{96,65},{97,1},{2,98}... | collective-permute-start | bytes 196616 | tf_op jit(solution)/shard_map/ppermute | solution.py:142
  22.4 0.0 collective-permute-done
  22.4 0.0 collective-permute-done.1
  22.5 0.8 collective-permute-done.2
  23.2 1.4 collective-permute-done.3
  24.6 0.7 pad_maximum_fusion.1
  25.4 0.0 all-gather.2.cloned.1.call-update
  25.4 1.2 copy.10
  26.6 41.0 %all_to_all.10.rows_ref = bf16[16,3,16,512]{3,2,1,0:T(8,128)(2,1)S(1)} all-to-all(bf16[16,3,16,512]{3,2,1,0:T(8,128)(2,1)S(1)} %bitcast.22), channel_id=1, replica_groups=mesh['x'=8,'yh'=2,'yl'=2,'core'=2,'Y'=2,'zz'=4,'par'=2] {'Y','zz','par'}, dimensions={0} | all-to-all | bytes 1572864 | tf_op jit(solution)/shard_map/all_to_all | solution.py:151
  67.7 1.9 %collective-permute-start.4 = (bf16[19,16,512]{2,1,0:T(8,128)(2,1)S(1)}, bf16[19,16,512]{2,1,0:T(8,128)(2,1)S(1)}, u32[]{:S(2)}, u32[]{:S(2)}) collective-permute-start(bf16[19,16,512]{2,1,0:T(8,128)(2,1)S(1)} %pad_maximum_fusion), channel_id=1, source_target_pairs={{0,16},{16,32},{32,48},{48,64},{64,80},{80,96},{96,112},{112,128},... | collective-permute-start | bytes 933896 | tf_op jit(solution)/shard_map/ppermute | solution.py:158
  69.6 0.0 copy-done.2
  69.7 0.4 shard_map.55.band_ref
  70.0 8.0 %collective-permute-done.4.halo_ref = bf16[19,16,512]{2,1,0:T(8,128)(2,1)S(1)} collective-permute-done((bf16[19,16,512]{2,1,0:T(8,128)(2,1)S(1)}, bf16[19,16,512]{2,1,0:T(8,128)(2,1)S(1)}, u32[]{:S(2)}, u32[]{:S(2)}) %collective-permute-start.4) | collective-permute-done | bytes 311328 | tf_op jit(solution)/shard_map/ppermute | solution.py:158
  78.1 0.0 copy-done.1
  78.1 2.1 %shard_map.56.own_ref = bf16[512,256]{1,0:T(8,128)(2,1)S(1)} custom-call(bf16[16,3,16,512]{3,2,1,0:T(8,128)(2,1)S(1)} %all_to_all.10.rows_ref, bf16[19,16,512]{2,1,0:T(8,128)(2,1)S(1)} %collective-permute-done.4.halo_ref, f32[3,7,512]{2,1,0:T(8,128)S(1)} %bitcast.20, bf16[32,256,128]{2,1,0:T(8,128)(2,1)S(1)} %shard_map.55.band_ref), custom_call_target="tpu_custom_call" | custom-call | flops 67108864 | bytes 3194880 | tf_op jit(solution)/shard_map/pallas_call | solution.py:172
  80.2 3.0 %collective-permute-start.5 = (bf16[512,256]{1,0:T(8,128)(2,1)S(1)}, bf16[512,256]{1,0:T(8,128)(2,1)S(1)}, u32[]{:S(2)}, u32[]{:S(2)}) collective-permute-start(bf16[512,256]{1,0:T(8,128)(2,1)S(1)} %shard_map.56.own_ref), channel_id=1, source_target_pairs={{0,1},{1,0},{2,3},{3,2},{4,5},{5,4},{6,7},{7,6},{8,9},{9,8},{10,11... | collective-permute-start | bytes 786440 | tf_op jit(solution)/shard_map/ppermute | solution.py:194
  83.3 0.0 all-gather.2.cloned.1.call-done
  83.3 2.2 %shard_map.57.weight_ref = bf16[8,2,2,2,64,512]{5,4,3,2,1,0:T(8,128)(2,1)S(1)} custom-call(bf16[8,2,2,2,64,512]{5,4,3,2,1,0:T(8,128)(2,1)} %bitcast.21), custom_call_target="tpu_custom_call" | custom-call | bytes 8388608 | tf_op jit(solution)/shard_map/pallas_call | solution.py:197
  85.5 0.0 copy-start
  85.6 5.5 %collective-permute-done.5.pair_ref = bf16[512,256]{1,0:T(8,128)(2,1)S(1)} collective-permute-done((bf16[512,256]{1,0:T(8,128)(2,1)S(1)}, bf16[512,256]{1,0:T(8,128)(2,1)S(1)}, u32[]{:S(2)}, u32[]{:S(2)}) %collective-permute-start.5) | collective-permute-done | bytes 262176 | tf_op jit(solution)/shard_map/ppermute | solution.py:194
  91.1 2.8 %shard_map.58 = bf16[8,256,256]{2,1,0:T(8,128)(2,1)} custom-call(s32[1]{0:T(128)} %bitcast.1.place_ref, bf16[512,256]{1,0:T(8,128)(2,1)S(1)} %shard_map.56.own_ref, bf16[512,256]{1,0:T(8,128)(2,1)S(1)} %collective-permute-done.5.pair_ref, bf16[8,2,2,2,64,512]{5,4,3,2,1,0:T(8,128)(2,1)S(1)} %shard_map.57.weight_ref), custom_call_target="tpu_custom_call" | custom-call | flops 1073741824 | bytes 5767168 | tf_op jit(solution)/shard_map/pallas_call | solution.py:209
  93.9 5.3 %all-to-all-start.1 = ((bf16[8,256,256]{2,1,0:T(8,128)(2,1)}), bf16[8,256,256]{2,1,0:T(8,128)(2,1)S(1)}, u32[]{:S(2)}, u32[]{:S(2)}) async-start(bf16[8,256,256]{2,1,0:T(8,128)(2,1)} %shard_map.58), calls=%async_computation.1 | async-start | bytes 2097152 | tf_op jit(solution)/shard_map/all_to_all | solution.py:226
  99.2 42.8 %all-to-all-done.1.parts_ref = bf16[8,256,256]{2,1,0:T(8,128)(2,1)S(1)} async-done(((bf16[8,256,256]{2,1,0:T(8,128)(2,1)}), bf16[8,256,256]{2,1,0:T(8,128)(2,1)S(1)}, u32[]{:S(2)}, u32[]{:S(2)}) %all-to-all-start.1) | async-done | bytes 1048608 | tf_op jit(solution)/shard_map/all_to_all | solution.py:226
  142.0 0.0 copy-done
  142.0 0.9 shard_map.59
  (3 shorter events, 0.1 us)
Async XLA Ops:
  6.5 63.1 %copy-start.2 = (f32[32,128]{1,0:T(8,128)S(1)}, f32[32,128]{1,0:T(8,128)}, u32[]{:S(2)}) copy-start(f32[32,128]{1,0:T(8,128)} %filter_ref.1) | copy-start | bytes 49156
  6.5 71.5 %copy-start.1 = (f32[7,3,512]{2,0,1:T(8,128)S(1)}, f32[7,3,512]{2,0,1:T(8,128)}, u32[]{:S(2)}) copy-start(f32[7,3,512]{2,0,1:T(8,128)} %param.6) | copy-start | bytes 129028
  6.5 76.8 %all-gather.2.cloned.1.call-start = ((), (), s32[]{:S(2)}) async-start(), calls=%async_computation.2 | async-start | bytes 4456448 | tf_op jit(solution)/shard_map/all_gather | solution.py:146
  6.5 15.9 %collective-permute-start = (bf16[64,512]{1,0:T(8,128)(2,1)}, bf16[64,512]{1,0:T(8,128)(2,1)S(1)}, u32[]{:S(2)}, u32[]{:S(2)}) collective-permute-start(bf16[64,512]{1,0:T(8,128)(2,1)} %bitcast.30), channel_id=1, source_target_pairs={{0,0},{1,64},{32,32},{33,96},{64,1},{65,65},{96,33},{97,97},{2,2},... | collective-permute-start | bytes 196616 | tf_op jit(solution)/shard_map/ppermute | solution.py:142
  11.4 11.0 %collective-permute-start.1 = (bf16[64,512]{1,0:T(8,128)(2,1)}, bf16[64,512]{1,0:T(8,128)(2,1)S(1)}, u32[]{:S(2)}, u32[]{:S(2)}) collective-permute-start(bf16[64,512]{1,0:T(8,128)(2,1)} %bitcast.31), channel_id=1, source_target_pairs={{0,32},{1,96},{32,0},{33,64},{64,33},{65,97},{96,1},{97,65},{2,34}... | collective-permute-start | bytes 196616 | tf_op jit(solution)/shard_map/ppermute | solution.py:142
  14.1 9.1 %collective-permute-start.2 = (bf16[64,512]{1,0:T(8,128)(2,1)}, bf16[64,512]{1,0:T(8,128)(2,1)S(1)}, u32[]{:S(2)}, u32[]{:S(2)}) collective-permute-start(bf16[64,512]{1,0:T(8,128)(2,1)} %bitcast.32), channel_id=1, source_target_pairs={{0,64},{1,0},{32,96},{33,32},{64,65},{65,1},{96,97},{97,33},{2,66}... | collective-permute-start | bytes 196616 | tf_op jit(solution)/shard_map/ppermute | solution.py:142
  16.0 8.6 %collective-permute-start.3 = (bf16[64,512]{1,0:T(8,128)(2,1)}, bf16[64,512]{1,0:T(8,128)(2,1)S(1)}, u32[]{:S(2)}, u32[]{:S(2)}) collective-permute-start(bf16[64,512]{1,0:T(8,128)(2,1)} %bitcast.33), channel_id=1, source_target_pairs={{0,96},{1,32},{32,64},{33,0},{64,97},{65,33},{96,65},{97,1},{2,98}... | collective-permute-start | bytes 196616 | tf_op jit(solution)/shard_map/ppermute | solution.py:142
  67.7 10.4 %collective-permute-start.4 = (bf16[19,16,512]{2,1,0:T(8,128)(2,1)S(1)}, bf16[19,16,512]{2,1,0:T(8,128)(2,1)S(1)}, u32[]{:S(2)}, u32[]{:S(2)}) collective-permute-start(bf16[19,16,512]{2,1,0:T(8,128)(2,1)S(1)} %pad_maximum_fusion), channel_id=1, source_target_pairs={{0,16},{16,32},{32,48},{48,64},{64,80},{80,96},{96,112},{112,128},... | collective-permute-start | bytes 933896 | tf_op jit(solution)/shard_map/ppermute | solution.py:158
  80.2 10.9 %collective-permute-start.5 = (bf16[512,256]{1,0:T(8,128)(2,1)S(1)}, bf16[512,256]{1,0:T(8,128)(2,1)S(1)}, u32[]{:S(2)}, u32[]{:S(2)}) collective-permute-start(bf16[512,256]{1,0:T(8,128)(2,1)S(1)} %shard_map.56.own_ref), channel_id=1, source_target_pairs={{0,1},{1,0},{2,3},{3,2},{4,5},{5,4},{6,7},{7,6},{8,9},{9,8},{10,11... | collective-permute-start | bytes 786440 | tf_op jit(solution)/shard_map/ppermute | solution.py:194
  85.5 56.5 %copy-start = (bf16[256,256]{1,0:T(8,128)(2,1)S(1)}, bf16[256,256]{1,0:T(8,128)(2,1)}, u32[]{:S(2)}) copy-start(bf16[256,256]{1,0:T(8,128)(2,1)} %residual_ref.1) | copy-start | bytes 393220
  93.9 48.2 %all-to-all-start.1 = ((bf16[8,256,256]{2,1,0:T(8,128)(2,1)}), bf16[8,256,256]{2,1,0:T(8,128)(2,1)S(1)}, u32[]{:S(2)}, u32[]{:S(2)}) async-start(bf16[8,256,256]{2,1,0:T(8,128)(2,1)} %shard_map.58), calls=%async_computation.1 | async-start | bytes 2097152 | tf_op jit(solution)/shard_map/all_to_all | solution.py:226
Sparse Core Ops, SparseCore 0:
  25.5 57.0 all-gather.1
